TPU v7x, 32 devices: a whole 2x2x4 slice. The times are simulated.
32 devices in a mesh: grp: 2 (over y), smp: 4 (over x, core), row: 4 (over z).
Axes of the slice: x: 2, y: 2, z: 4, core: 2. Of those that a mesh axis runs over, the one named last changes fastest.
Arguments:
- positions: float32 [8, 3, 4096], P(('grp', 'smp'), None, 'row'), parts along dimension 0, may hold values from -60 to 60
- noise_draw: float32 [8, 3, 4096], P(('grp', 'smp'), None, 'row'), parts along dimension 0, may hold values from -6 to 6
- noise_level: float32 [8], P(('grp', 'smp')), parts along dimension 0, may hold values from 0.5 to 80
- atom_single: bfloat16 [8192, 128], P(('grp', 'row')), parts along dimension 0, may hold values from -6 to 6
- token_single: bfloat16 [1024, 768], P(('grp', 'row')), parts along dimension 0, may hold values from -6 to 6
- pair_cond: bfloat16 [1024, 512, 128], P(('grp', 'row'), 'smp'), parts along dimension 0, may hold values from -6 to 6
- atom_to_token: int32 [8192], P(('grp', 'row')), parts along dimension 0, may hold values from 0 to 511, as said below
- window_offsets: int32 [256], P(('grp', 'row')), parts along dimension 0, may hold values from -96 to 0
- atom_mask: int32 [8192], P('grp'), parts along dimension 0, may hold values 0 or 1
- token_mask: int32 [1024], P('grp'), parts along dimension 0, may hold values 0 or 1
- coord_in: float32 [3, 128], replicated, may hold values from -3.5 to 3.5
- atom_gain: float32 [2, 128], replicated, may hold values from 0.1 to 1.9
- atom_qkv: bfloat16 [2, 128, 384], replicated, may hold values from -1 to 1
- atom_proj: bfloat16 [2, 128, 128], replicated, may hold values from -0.5 to 0.5
- gather_in: bfloat16 [128, 768], replicated, may hold values from -0.5 to 0.5
- noise_embed: float32 [768], replicated, may hold values from -6 to 6
- pair_gain: float32 [128], replicated, may hold values from 0.1 to 1.9
- pair_heads: bfloat16 [128, 16], replicated, may hold values from -0.5 to 0.5
- token_gain: float32 [2, 768], replicated, may hold values from 0.1 to 1.9
- token_qkv: bfloat16 [768, 2304], replicated, may hold values from -1 to 1
- token_proj: bfloat16 [768, 768], replicated, may hold values from -0.21875 to 0.21875
- ffn_in: bfloat16 [768, 3072], replicated, may hold values from -0.21875 to 0.21875
- ffn_out: bfloat16 [1536, 768], replicated, may hold values from -0.15625 to 0.15625
- scatter_out: bfloat16 [768, 128], replicated, may hold values from -0.21875 to 0.21875
- out_gain: float32 [128], replicated, may hold values from 0.1 to 1.9
- coord_out: bfloat16 [3, 128], replicated, may hold values from -0.5 to 0.5
Outputs:
- token_out: bfloat16 [8, 512, 768], P(('grp', 'smp'), 'row'), parts along dimension 0
- direction: float32 [8, 3, 4096], P(('grp', 'smp'), None, 'row'), parts along dimension 0
There are 2 independent parts, one for each index of `grp`. A program takes and returns all parts, laid end to end along the dimension named above; an argument that names none is the same for every part. Nothing has to cross between parts.
Inputs may be any that keep to these rules, and one draw needn't show every extreme that they name: `atom_to_token`: never falls along the atoms; atoms k * 1024 to (k + 1) * 1024 - 1 belong to tokens k * 128 to (k + 1) * 128 - 1; some tokens have no atom.
All inputs are finite; a program needn't handle non-finite values.
Results may differ from a plain program's by a relative error of at most 0.013.
Values may be sent and summed in bfloat16 or wider, within the bound.
A program may use at most 128 MiB of HBM per device.

v0:
```python
import jax
import jax.numpy as jnp
from jax import lax
from jax.sharding import PartitionSpec as P

D = 768
HEADS = 16
FF = 1536
CA = 128
AHEADS = 4
WQ = 32
WK = 128
HALO = 96


sigma_data = 16.0
gamma_boost = 0.8
norm_eps = 1e-05
masked_score = -1e30
outside_score = -2e30


def with_halo(block, sides, width):
    for axis, dim in sides:
        count = lax.axis_size(axis)
        forward = [(i, i + 1) for i in range(count - 1)]
        backward = [(target, source) for source, target in forward]
        low = lax.ppermute(
            lax.slice_in_dim(block, block.shape[dim] - width, None, axis=dim), axis, forward
        )
        high = lax.ppermute(lax.slice_in_dim(block, 0, width, axis=dim), axis, backward)
        block = jnp.concatenate([low, block, high], axis=dim)
    return block


def layer_norm(values, norm_gain):
    average = jnp.mean(values, axis=-1, keepdims=True)
    centred = values - average
    variance = jnp.mean(centred * centred, axis=-1, keepdims=True)
    return centred * lax.rsqrt(variance + norm_eps) * norm_gain


def softmax_rows(scores):
    largest = jnp.max(scores, axis=-1, keepdims=True)
    exponent = jnp.exp(scores - largest)
    return exponent / jnp.sum(exponent, axis=-1, keepdims=True)


def pair_bias_of(pair_tile, pair_gain, pair_heads):
    normed = layer_norm(pair_tile.astype(jnp.float32), pair_gain).astype(jnp.bfloat16)
    return jnp.einsum("ijc,ch->hij", normed, pair_heads, preferred_element_type=jnp.float32).astype(
        jnp.bfloat16
    )


def block_spans(extended, block_count, span_blocks):
    tail_shape = extended.shape[1:]
    grouped = extended.reshape((block_count + span_blocks - 1, WQ) + tail_shape)
    pieces = [grouped[shift : shift + block_count] for shift in range(span_blocks)]
    return jnp.stack(pieces, axis=1).reshape((block_count, span_blocks * WQ) + tail_shape)


def window_attend(queries, windows, live, inside, w_out):
    block_count = queries.shape[0] // WQ
    head_size = CA // AHEADS
    span_rows = windows.shape[1]
    query_heads = queries.reshape(block_count, WQ, AHEADS, head_size)
    key_heads = windows[:, :, :CA].reshape(block_count, span_rows, AHEADS, head_size)
    value_heads = windows[:, :, CA:].reshape(block_count, span_rows, AHEADS, head_size)
    scores = jnp.einsum(
        "bqhd,bkhd->bhqk", query_heads, key_heads, preferred_element_type=jnp.float32
    ) / jnp.sqrt(jnp.float32(head_size))
    scores = jnp.where(live[:, None, None, :], scores, masked_score)
    scores = jnp.where(inside[:, None, None, :], scores, outside_score)
    weights = softmax_rows(scores).astype(jnp.bfloat16)
    mixed_heads = jnp.einsum(
        "bhqk,bkhd->bqhd", weights, value_heads, preferred_element_type=jnp.float32
    ).astype(jnp.bfloat16)
    return jnp.dot(
        mixed_heads.reshape(block_count * WQ, CA), w_out, preferred_element_type=jnp.float32
    )


def atom_block(atom_state, norm_gain, w_qkv, w_out, offsets, live_ext):
    row_count = atom_state.shape[0]
    normed = layer_norm(atom_state, norm_gain).astype(jnp.bfloat16)
    widened = with_halo(normed, (("row", 0),), HALO)
    projected = jnp.dot(widened, w_qkv, preferred_element_type=jnp.float32).astype(jnp.bfloat16)
    queries = projected[HALO : HALO + row_count, :CA]
    extended = projected[:, CA:]
    block_count = row_count // WQ
    span_blocks = (2 * HALO + WQ) // WQ
    windows = block_spans(extended, block_count, span_blocks)
    live = block_spans(live_ext, block_count, span_blocks) > 0
    relative = jnp.arange(span_blocks * WQ, dtype=jnp.int32)[None, :]
    first_key = offsets[:, None] + HALO
    inside = (relative >= first_key) & (relative < first_key + WK)
    return atom_state + window_attend(queries, windows, live, inside, w_out)


def per_device(
    positions,
    noise_draw,
    noise_level,
    atom_single,
    token_single,
    pair_cond,
    atom_to_token,
    window_offsets,
    atom_mask,
    token_mask,
    coord_in,
    atom_gain,
    atom_qkv,
    atom_proj,
    gather_in,
    noise_embed,
    pair_gain,
    pair_heads,
    token_gain,
    token_qkv,
    token_proj,
    ffn_in,
    ffn_out,
    scatter_out,
    out_gain,
    coord_out,
):
    row_index = lax.axis_index("row")
    tok_rows = token_single.shape[0]
    atom_rows = atom_single.shape[0]
    head_size = D // HEADS
    biases = lax.all_gather(
        pair_bias_of(pair_cond, pair_gain, pair_heads), "smp", axis=2, tiled=True
    )
    local_token = atom_to_token - row_index * tok_rows
    valid_local = lax.dynamic_slice_in_dim(atom_mask, row_index * atom_rows, atom_rows)
    member = (local_token[None, :] == jnp.arange(tok_rows, dtype=jnp.int32)[:, None]) & (
        valid_local[None, :] > 0
    )
    onehot = member.astype(jnp.bfloat16)
    counts = jnp.maximum(jnp.sum(member.astype(jnp.float32), axis=1), 1.0)
    live_padded = jnp.pad(atom_mask, (HALO, HALO))
    live_ext = lax.dynamic_slice_in_dim(live_padded, row_index * atom_rows, atom_rows + 2 * HALO)
    key_live = token_mask > 0
    coords = positions[0]
    kicks = noise_draw[0]
    level_now = noise_level[0]
    level_hat = (1.0 + gamma_boost) * level_now
    noisy = coords + jnp.sqrt(level_hat * level_hat - level_now * level_now) * kicks
    scaled = noisy / jnp.sqrt(level_hat * level_hat + sigma_data * sigma_data)
    atom_state = atom_single.astype(jnp.float32) + jnp.einsum(
        "ka,kc->ac", scaled, coord_in, precision=lax.Precision.HIGHEST
    )
    atom_state = atom_block(
        atom_state, atom_gain[0], atom_qkv[0], atom_proj[0], window_offsets, live_ext
    )
    lifted = jax.nn.relu(
        jnp.dot(atom_state.astype(jnp.bfloat16), gather_in, preferred_element_type=jnp.float32)
    ).astype(jnp.bfloat16)
    pooled = jnp.dot(onehot, lifted, preferred_element_type=jnp.float32) / counts[:, None]
    token_state = (
        pooled
        + token_single.astype(jnp.float32)
        + jnp.log(level_hat / sigma_data) / 4.0 * noise_embed
    )
    normed = layer_norm(token_state, token_gain[0]).astype(jnp.bfloat16)
    projected = jnp.dot(normed, token_qkv, preferred_element_type=jnp.float32).astype(jnp.bfloat16)
    gathered = lax.all_gather(projected[:, D:], "row", axis=0, tiled=True)
    key_count = gathered.shape[0]
    query_heads = projected[:, :D].reshape(tok_rows, HEADS, head_size)
    key_heads = gathered[:, :D].reshape(key_count, HEADS, head_size)
    value_heads = gathered[:, D:].reshape(key_count, HEADS, head_size)
    scores = jnp.einsum(
        "ihd,jhd->hij", query_heads, key_heads, preferred_element_type=jnp.float32
    ) / jnp.sqrt(jnp.float32(head_size))
    scores = scores + biases.astype(jnp.float32)
    scores = jnp.where(key_live[None, None, :], scores, masked_score)
    weights = softmax_rows(scores).astype(jnp.bfloat16)
    mixed_heads = (
        jnp.einsum("hij,jhd->ihd", weights, value_heads, preferred_element_type=jnp.float32)
        .astype(jnp.bfloat16)
        .reshape(tok_rows, D)
    )
    token_state = token_state + jnp.dot(mixed_heads, token_proj, preferred_element_type=jnp.float32)
    normed = layer_norm(token_state, token_gain[1]).astype(jnp.bfloat16)
    hidden = jnp.dot(normed, ffn_in, preferred_element_type=jnp.float32)
    active = (jax.nn.silu(hidden[:, :FF]) * hidden[:, FF:]).astype(jnp.bfloat16)
    token_state = token_state + jnp.dot(active, ffn_out, preferred_element_type=jnp.float32)
    token_result = token_state.astype(jnp.bfloat16)
    spread_back = jnp.dot(token_result, scatter_out, preferred_element_type=jnp.float32).astype(
        jnp.bfloat16
    )
    atom_state = atom_state + lax.dot_general(
        onehot, spread_back, (((0,), (0,)), ((), ())), preferred_element_type=jnp.float32
    )
    atom_state = atom_block(
        atom_state, atom_gain[1], atom_qkv[1], atom_proj[1], window_offsets, live_ext
    )
    normed_out = layer_norm(atom_state, out_gain).astype(jnp.bfloat16)
    update = lax.dot_general(
        coord_out, normed_out, (((1,), (1,)), ((), ())), preferred_element_type=jnp.float32
    )
    base_square = sigma_data * sigma_data + level_hat * level_hat
    skip_scale = sigma_data * sigma_data / base_square
    out_scale = level_hat * sigma_data / jnp.sqrt(base_square)
    denoised = skip_scale * noisy + out_scale * update
    direction = (noisy - denoised) / level_hat
    return (token_result[None], direction[None])


def solution(mesh):
    in_specs = (
        P(("grp", "smp"), None, "row"),
        P(("grp", "smp"), None, "row"),
        P(("grp", "smp")),
        P(("grp", "row"), None),
        P(("grp", "row"), None),
        P(("grp", "row"), "smp", None),
        P(("grp", "row")),
        P(("grp", "row")),
        P("grp"),
        P("grp"),
        P(),
        P(),
        P(),
        P(),
        P(),
        P(),
        P(),
        P(),
        P(),
        P(),
        P(),
        P(),
        P(),
        P(),
        P(),
        P(),
    )
    out_specs = (P(("grp", "smp"), "row", None), P(("grp", "smp"), None, "row"))
    return jax.shard_map(
        per_device, mesh=mesh, in_specs=in_specs, out_specs=out_specs, check_vma=False
    )
```

profile of v0, /device:TPU:0, one launch (start us, length us, event | category | flops | bytes accessed | tf_op | source)
XLA Modules:
  0.0 203.9 jit_solution(14690072002025671553)
XLA Ops:
  8.1 2.2 %fusion.123 = (f32[1024]{0:T(1024)S(1)}, f32[1024,128]{1,0:T(8,128)S(1)}) fusion(f32[3,128]{1,0:T(4,128)} %param.36, f32[]{:T(128)S(6)} %sqrt.8, f32[1,3,1024]{2,0,1:T(1,128)} %param.27, f32[]{:T(128)S(6)} %sqrt.7, f32[1,3,1024]{2,0,1:T(1,128)} %param.26, bf16[1024,128]{1,0:T(8,128)(2,1)} %param.29), kind=kOutput, calls=%fused_computation.202 | convolution fusion | flops 5120000 | bytes 816648 | tf_op jit(solution)/shard_map/ka,kc->ac/dot_general | solution.py:152
  10.7 1.3 slice_bitcast_fusion
  12.4 0.7 copy-done.10
  13.7 5.6 %collective-permute-start = (bf16[96,128]{1,0:T(8,128)(2,1)}, bf16[96,128]{1,0:T(8,128)(2,1)}, u32[]{:S(2)}, u32[]{:S(2)}) collective-permute-start(bf16[96,128]{1,0:T(8,128)(2,1)} %get-tuple-element.32), channel_id=1, source_target_pairs={{0,1},{1,2},{2,3},{4,5},{5,6},{6,7},{8,9},{9,10},{10,11},{12,13},{... | collective-permute-start | bytes 73736 | tf_op jit(solution)/shard_map/ppermute | solution.py:28
  19.3 1.3 collective-permute-start.1
  20.6 1.7 pad_dynamic-slice_fusion.6
  22.2 0.8 stack.88
  23.0 1.4 stack.89
  24.4 1.4 stack.90
  25.7 1.4 stack.91
  27.1 1.4 stack.92
  28.5 1.4 stack.93
  29.8 1.4 stack.94
  31.2 1.6 stack.95
  32.8 1.5 broadcast_compare_fusion
  34.3 0.7 broadcast_add_fusion.1
  35.0 0.7 dynamic-slice_compare_fusion
  35.7 0.7 broadcast_subtract_fusion
  37.1 0.7 fusion.94
  37.8 1.3 broadcast_multiply_fusion.1
  39.1 0.8 slice_reduce_fusion
  39.9 1.5 gt.27
  41.4 1.4 convolution_convert_fusion.2
  43.0 0.7 slice.290
  44.1 2.5 %fusion.117 = (bf16[32,224,128]{2,1,0:T(8,128)(2,1)}, bf16[32,224,128]{2,1,0:T(8,128)(2,1)}) fusion(bf16[32,224,256]{2,1,0:T(8,128)(2,1)S(1)} %bitcast.141), kind=kLoop, calls=%fused_computation.196 | loop fusion | bytes 7340032 | tf_op jit(solution)/shard_map/slice | solution.py:68
  46.5 4.0 %copy.78 = bf16[32,224,128]{1,2,0:T(8,128)(2,1)} copy(bf16[32,224,128]{2,1,0:T(8,128)(2,1)} %get-tuple-element.12) | data formatting | bytes 3670016 | tf_op jit(solution)/shard_map/slice | solution.py:68
  50.5 2.7 %reshape.297 = bf16[32,32,4,32]{3,2,1,0:T(4,128)(2,1)} reshape(bf16[1024,128]{1,0:T(8,128)(2,1)} %slice.290) | data formatting | bytes 524288 | tf_op jit(solution)/shard_map/reshape | solution.py:67
  53.3 3.9 %copy.77 = bf16[32,224,128]{1,2,0:T(8,128)(2,1)} copy(bf16[32,224,128]{2,1,0:T(8,128)(2,1)} %get-tuple-element.13) | data formatting | bytes 3670016 | tf_op jit(solution)/shard_map/slice | solution.py:69
  57.2 2.6 %fusion.49 = f32[32,4,32,224]{3,2,1,0:T(8,128)S(1)} fusion(bf16[32,224,4,32]{1,3,2,0:T(8,128)(2,1)} %bitcast.139, bf16[32,32,4,32]{3,2,1,0:T(4,128)(2,1)} %reshape.297), kind=kOutput, calls=%fused_computation.72 | convolution fusion | flops 58720256 | bytes 5767168 | tf_op jit(solution)/shard_map/bqhd,bkhd->bhqk/dot_general | solution.py:70
  59.9 6.4 %fusion.124 = (f32[32,4,32]{2,1,0:T(4,128)S(1)}, f32[32,4,32,224]{3,2,1,0:T(8,128)S(1)}) fusion(f32[32,4,32,224]{3,2,1,0:T(8,128)S(1)} %fusion.49, pred[32,224]{1,0:T(8,128)(4,1)S(1)} %copy-done.17, pred[32,224]{1,0:T(8,128)(4,1)S(1)} %copy-done.19), kind=kOutput, calls=%fused_computation.203 | output fusion | flops 7340255 | bytes 7370752 | tf_op jit(solution)/shard_map/sub | solution.py:45
  66.3 1.0 fusion.35
  67.3 1.7 copy.80
  69.0 2.9 %reshape.299 = bf16[1024,128]{0,1:T(8,128)(2,1)} reshape(bf16[32,32,4,32]{1,0,3,2:T(8,128)(2,1)} %copy.80) | data formatting | bytes 524288 | tf_op jit(solution)/shard_map/reshape | solution.py:80
  71.9 2.2 %convolution_add_fusion.2 = f32[1024,128]{1,0:T(8,128)} fusion(f32[1024,128]{1,0:T(8,128)} %copy-done.3, bf16[1024,128]{0,1:T(8,128)(2,1)} %reshape.299, bf16[2,128,128]{2,1,0:T(8,128)(2,1)} %param.39), kind=kOutput, calls=%fused_computation.53 | convolution fusion | flops 33685504 | bytes 1343488 | tf_op jit(solution)/shard_map/dot_general | solution.py:79
  74.1 3.3 %fusion.125 = (f32[128]{0:T(128)}, f32[128,768]{1,0:T(8,128)}) fusion(f32[768]{0:T(1024)} %broadcast_multiply_fusion.1, bf16[128,768]{1,0:T(8,128)(2,1)} %param.30, f32[128]{0:T(128)} %broadcast_maximum_fusion, bf16[128,768]{1,0:T(8,128)(2,1)} %param.40, f32[1024,128]{1,0:T(8,128)} %convolution_add_fusion.2, s32[1024]{0:T(1024)S(1)} %broadcast_subtract_fusion, ...), kind=kOutput, calls=%fused_computation.204 | convolution fusion | flops 405110656 | bytes 1319936 | tf_op jit(solution)/shard_map/dot_general | solution.py:161
  77.5 0.7 broadcast_multiply_fusion.6
  78.1 1.2 multiply_reduce_fusion.4
  79.3 1.7 convolution_convert_fusion
  81.0 0.8 copy-done.7
  81.8 0.8 slice.292
  82.9 3.5 %convert_reduce_fusion = f32[128,128]{1,0:T(8,128)S(1)} fusion(bf16[128,128,128]{2,1,0:T(8,128)(2,1)} %param.31), kind=kLoop, calls=%fused_computation.4 | loop fusion | flops 4177920 | bytes 4259840 | tf_op jit(solution)/shard_map/reduce_sum | solution.py:37
  86.5 4.8 %fusion.5 = f32[128,128]{1,0:T(8,128)S(1)} fusion(bf16[128,128,128]{2,1,0:T(8,128)(2,1)S(1)} %copy-done.2, f32[128,128]{1,0:T(8,128)S(1)} %broadcast_multiply_fusion), kind=kLoop, calls=%fused_computation.7 | loop fusion | flops 8372224 | bytes 4325376 | tf_op jit(solution)/shard_map/reduce_sum | solution.py:39
  91.3 5.8 %fusion.8 = bf16[128,128,16]{1,2,0:T(8,128)(2,1)S(1)} fusion(bf16[128,128,128]{2,1,0:T(8,128)(2,1)S(1)} %copy-done.2, f32[128]{0:T(128)S(1)} %copy-done.27, f32[128,128]{1,0:T(8,128)S(1)} %add_rsqrt_fusion, f32[128,128]{1,0:T(8,128)S(1)} %broadcast_multiply_fusion, bf16[128,16]{0,1:T(8,128)(2,1)S(1)} %copy-done.25), kind=kOutput, calls=%fused_computation.10 | convolution fusion | flops 77594624 | bytes 4854272 | tf_op jit(solution)/shard_map/ijc,ch->hij/dot_general | solution.py:51
  97.2 1.0 copy.124
  98.4 23.7 %all-gather.3.cloned.1.call-done = bf16[512,1536]{1,0:T(8,128)(2,1)} async-done(((bf16[128,1536]{1,0:T(8,128)(2,1)}), bf16[512,1536]{1,0:T(8,128)(2,1)}) %all-gather.3.cloned.1.call-update) | async-done | bytes 1572880 | tf_op jit(solution)/shard_map/all_gather | solution.py:169
  122.1 1.5 fusion.118
  124.1 21.2 %all-gather.5.cloned.1.call-done = bf16[16,128,512]{2,1,0:T(8,128)(2,1)} async-done(((bf16[16,128,128]{2,1,0:T(8,128)(2,1)}), bf16[16,128,512]{2,1,0:T(8,128)(2,1)}) %all-gather.5.cloned.1.call-update) | async-done | bytes 2097168 | tf_op jit(solution)/shard_map/all_gather | solution.py:133
  145.4 3.3 %fusion.128 = f32[16,128]{1,0:T(8,128)S(1)} fusion(bf16[16,128,512]{2,1,0:T(8,128)(2,1)} %all-gather.5.cloned.1.call-done, pred[512]{0:T(512)(128)(4,1)S(1)} %broadcast_compare_fusion.1, bf16[128,16,48]{0,2,1:T(8,128)(2,1)S(1)} %bitcast.165, bf16[512,16,48]{0,2,1:T(8,128)(2,1)S(1)} %bitcast.160), kind=kOutput, calls=%fused_computation.205 | convolution fusion | flops 106955264 | bytes 3088896 | tf_op jit(solution)/shard_map/sub | solution.py:45
  148.8 4.5 %fusion.40 = bf16[16,48,128]{2,1,0:T(8,128)(2,1)} fusion(bf16[512,16,48]{0,2,1:T(8,128)(2,1)S(1)} %bitcast.162, f32[16,128]{1,0:T(8,128)S(1)} %fusion.128, bf16[16,128,512]{2,1,0:T(8,128)(2,1)} %all-gather.5.cloned.1.call-done, pred[512]{0:T(512)(128)(4,1)} %copy-done.23, bf16[128,16,48]{0,2,1:T(8,128)(2,1)} %bitcast.166, bf16[512,16,48]{0,2,1:T(8,128)(2,1)S(1)} %bitcast.161), kind=kOutput, calls=%fused_computation.60 | convolution fusion | flops 208767488 | bytes 4071936 | tf_op jit(solution)/shard_map/hij,jhd->ihd/dot_general | solution.py:181
  153.3 1.4 fusion.129
  154.9 3.3 %fusion.79 = f32[128,3072]{1,0:T(8,128)S(1)} fusion(bf16[768,3072]{1,0:T(8,128)(2,1)} %param.47, f32[128,768]{1,0:T(8,128)S(1)} %get-tuple-element.52, f32[768]{0:T(1024)S(1)} %get-tuple-element.8, f32[128]{0:T(128)S(1)} %add_rsqrt_fusion.4, f32[128]{0:T(128)S(1)} %broadcast_multiply_fusion.5), kind=kOutput, calls=%fused_computation.110 | convolution fusion | flops 604372992 | bytes 6688768 | tf_op jit(solution)/shard_map/dot_general | solution.py:187
  160.6 3.4 %collective-permute-start.2 = (bf16[96,128]{1,0:T(8,128)(2,1)S(1)}, bf16[96,128]{1,0:T(8,128)(2,1)S(1)}, u32[]{:S(2)}, u32[]{:S(2)}) collective-permute-start(bf16[96,128]{1,0:T(8,128)(2,1)S(1)} %get-tuple-element.30), channel_id=1, source_target_pairs={{0,1},{1,2},{2,3},{4,5},{5,6},{6,7},{8,9},{9,10},{10,11},{12,13},{... | collective-permute-start | bytes 73736 | tf_op jit(solution)/shard_map/ppermute | solution.py:28
  164.0 1.5 collective-permute-start.3
  165.6 4.1 %collective-permute-done.3 = bf16[96,128]{1,0:T(8,128)(2,1)S(1)} collective-permute-done((bf16[96,128]{1,0:T(8,128)(2,1)S(1)}, bf16[96,128]{1,0:T(8,128)(2,1)S(1)}, u32[]{:S(2)}, u32[]{:S(2)}) %collective-permute-start.3) | collective-permute-done | bytes 24608 | tf_op jit(solution)/shard_map/ppermute | solution.py:31
  170.7 2.5 %fusion.116 = (bf16[32,224,128]{2,1,0:T(8,128)(2,1)}, bf16[32,224,128]{2,1,0:T(8,128)(2,1)}) fusion(bf16[32,224,256]{2,1,0:T(8,128)(2,1)S(1)} %bitcast.142), kind=kLoop, calls=%fused_computation.195 | loop fusion | bytes 7340032 | tf_op jit(solution)/shard_map/slice | solution.py:68
  173.2 3.2 %copy.93 = bf16[32,224,128]{1,2,0:T(8,128)(2,1)S(1)} copy(bf16[32,224,128]{2,1,0:T(8,128)(2,1)} %get-tuple-element.10) | data formatting | bytes 3670016 | tf_op jit(solution)/shard_map/slice | solution.py:68
  176.8 0.7 fusion.47
  177.5 4.3 %fusion.131 = (f32[32,4,32]{2,1,0:T(4,128)}, f32[32,4,32,224]{3,2,1,0:T(8,128)}) fusion(f32[32,4,32,224]{3,2,1,0:T(8,128)S(1)} %fusion.47, pred[32,224]{1,0:T(8,128)(4,1)S(1)} %copy-done.18, pred[32,224]{1,0:T(8,128)(4,1)S(1)} %copy-done.20), kind=kOutput, calls=%fused_computation.208 | output fusion | flops 7340255 | bytes 7370752 | tf_op jit(solution)/shard_map/sub | solution.py:45
  181.8 3.1 %copy.92 = bf16[32,224,128]{1,2,0:T(8,128)(2,1)} copy(bf16[32,224,128]{2,1,0:T(8,128)(2,1)S(1)} %copy-done.5) | data formatting | bytes 3670016 | tf_op jit(solution)/shard_map/slice | solution.py:69
  184.9 3.8 %fusion.36 = bf16[32,32,4,32]{1,3,2,0:T(8,128)(2,1)S(1)} fusion(bf16[32,224,4,32]{1,3,2,0:T(8,128)(2,1)} %bitcast.159, f32[32,4,32,224]{3,2,1,0:T(8,128)} %get-tuple-element.56, f32[32,4,32]{2,1,0:T(4,128)} %get-tuple-element.55), kind=kOutput, calls=%fused_computation.50 | convolution fusion | flops 60686336 | bytes 5783552 | tf_op jit(solution)/shard_map/bhqk,bkhd->bqhd/dot_general | solution.py:76
  188.7 1.7 copy.95
  190.4 2.9 %reshape.308 = bf16[1024,128]{0,1:T(8,128)(2,1)} reshape(bf16[32,32,4,32]{1,0,3,2:T(8,128)(2,1)} %copy.95) | data formatting | bytes 524288 | tf_op jit(solution)/shard_map/reshape | solution.py:80
  193.3 1.6 fusion.132
  195.3 1.2 fusion.46
  (110 shorter events, 8.6 us)
Async XLA Ops:
  7.2 72.2 %copy-start = (bf16[768,2304]{1,0:T(8,128)(2,1)S(1)}, bf16[768,2304]{1,0:T(8,128)(2,1)}, u32[]{:S(2)}) copy-start(bf16[768,2304]{1,0:T(8,128)(2,1)} %param.45) | copy-start | bytes 10616836
  7.2 114.9 %all-gather.3.cloned.1.call-start = ((), (), s32[]{:S(2)}) async-start(), calls=%async_computation | async-start | bytes 1966080 | tf_op jit(solution)/shard_map/all_gather | solution.py:169
  10.3 1.7 copy-start.3
  12.4 0.7 copy-start.10
  13.7 27.7 %collective-permute-start = (bf16[96,128]{1,0:T(8,128)(2,1)}, bf16[96,128]{1,0:T(8,128)(2,1)}, u32[]{:S(2)}, u32[]{:S(2)}) collective-permute-start(bf16[96,128]{1,0:T(8,128)(2,1)} %get-tuple-element.32), channel_id=1, source_target_pairs={{0,1},{1,2},{2,3},{4,5},{5,6},{6,7},{8,9},{9,10},{10,11},{12,13},{... | collective-permute-start | bytes 73736 | tf_op jit(solution)/shard_map/ppermute | solution.py:28
  19.3 22.1 %collective-permute-start.1 = (bf16[96,128]{1,0:T(8,128)(2,1)}, bf16[96,128]{1,0:T(8,128)(2,1)}, u32[]{:S(2)}, u32[]{:S(2)}) collective-permute-start(bf16[96,128]{1,0:T(8,128)(2,1)} %get-tuple-element.33), channel_id=1, source_target_pairs={{1,0},{2,1},{3,2},{5,4},{6,5},{7,6},{9,8},{10,9},{11,10},{13,12},{... | collective-permute-start | bytes 73736 | tf_op jit(solution)/shard_map/ppermute | solution.py:31
  57.2 2.6 %copy-start.17 = (pred[32,224]{1,0:T(8,128)(4,1)S(1)}, pred[32,224]{1,0:T(8,128)(4,1)}, u32[]{:S(2)}) copy-start(pred[32,224]{1,0:T(8,128)(4,1)} %gt.27) | copy-start | bytes 21508
  57.2 2.6 %copy-start.19 = (pred[32,224]{1,0:T(8,128)(4,1)S(1)}, pred[32,224]{1,0:T(8,128)(4,1)}, u32[]{:S(2)}) copy-start(pred[32,224]{1,0:T(8,128)(4,1)} %fusion.94) | copy-start | bytes 21508
  59.9 6.4 %copy-start.8 = (bf16[32,224,128]{1,2,0:T(8,128)(2,1)S(1)}, bf16[32,224,128]{1,2,0:T(8,128)(2,1)}, u32[]{:S(2)}) copy-start(bf16[32,224,128]{1,2,0:T(8,128)(2,1)} %copy.77) | copy-start | bytes 5505028
  81.0 0.8 copy-start.7
  82.7 8.6 %copy-start.25 = (bf16[128,16]{0,1:T(8,128)(2,1)S(1)}, bf16[128,16]{0,1:T(8,128)(2,1)}, u32[]{:S(2)}) copy-start(bf16[128,16]{0,1:T(8,128)(2,1)} %param.43) | copy-start | bytes 12292
  82.7 8.6 %copy-start.27 = (f32[128]{0:T(128)S(1)}, f32[128]{0:T(128)}, u32[]{:S(2)}) copy-start(f32[128]{0:T(128)} %param.42) | copy-start | bytes 1540
  82.7 62.7 %all-gather.5.cloned.1.call-start = ((), (), s32[]{:S(2)}) async-start(), calls=%async_computation.1 | async-start | bytes 2621440 | tf_op jit(solution)/shard_map/all_gather | solution.py:133
  82.9 3.5 %copy-start.2 = (bf16[128,128,128]{2,1,0:T(8,128)(2,1)S(1)}, bf16[128,128,128]{2,1,0:T(8,128)(2,1)}, u32[]{:S(2)}) copy-start(bf16[128,128,128]{2,1,0:T(8,128)(2,1)} %param.31) | copy-start | bytes 12582916
  91.3 6.9 %copy-start.21 = (s32[512]{0:T(512)S(1)}, s32[512]{0:T(512)}, u32[]{:S(2)}) copy-start(s32[512]{0:T(512)} %param.35) | copy-start | bytes 6148
  91.3 6.9 %slice-start = ((bf16[128,2304]{1,0:T(8,128)(2,1)}), bf16[128,768]{1,0:T(8,128)(2,1)S(1)}, s32[]{:S(2)}) async-start(bf16[128,2304]{1,0:T(8,128)(2,1)} %copy-done.7), calls=%async_computation.2 | async-start | bytes 393216 | tf_op jit(solution)/shard_map/slice | solution.py:171
  98.2 50.6 %copy-start.23 = (pred[512]{0:T(512)(128)(4,1)}, pred[512]{0:T(512)(128)(4,1)S(1)}, u32[]{:S(2)}) copy-start(pred[512]{0:T(512)(128)(4,1)S(1)} %broadcast_compare_fusion.1) | copy-start | bytes 1540
  98.3 50.4 %copy-start.14 = (bf16[128,768]{0,1:T(8,128)(2,1)}, bf16[128,768]{0,1:T(8,128)(2,1)S(1)}, u32[]{:S(2)}) copy-start(bf16[128,768]{0,1:T(8,128)(2,1)S(1)} %copy.82) | copy-start | bytes 589828
  148.7 4.5 %copy-start.6 = (f32[128,768]{1,0:T(8,128)S(1)}, f32[128,768]{1,0:T(8,128)}, u32[]{:S(2)}) copy-start(f32[128,768]{1,0:T(8,128)} %get-tuple-element.50) | copy-start | bytes 1179652
  148.8 4.5 %copy-start.11 = (bf16[768,768]{1,0:T(8,128)(2,1)S(1)}, bf16[768,768]{1,0:T(8,128)(2,1)}, u32[]{:S(2)}) copy-start(bf16[768,768]{1,0:T(8,128)(2,1)} %param.46) | copy-start | bytes 3538948
  154.6 3.5 %copy-start.24 = (bf16[1536,768]{1,0:T(8,128)(2,1)S(1)}, bf16[1536,768]{1,0:T(8,128)(2,1)}, u32[]{:S(2)}) copy-start(bf16[1536,768]{1,0:T(8,128)(2,1)} %param.48) | copy-start | bytes 7077892
  158.2 1.0 copy-start.9
  158.2 1.1 copy-start.12
  158.2 2.0 copy-start.22
  158.2 11.5 %copy-start.15 = (bf16[2,128,384]{2,1,0:T(8,128)(2,1)S(1)}, bf16[2,128,384]{2,1,0:T(8,128)(2,1)}, u32[]{:S(2)}) copy-start(bf16[2,128,384]{2,1,0:T(8,128)(2,1)} %param.38) | copy-start | bytes 589828
  159.3 10.8 %copy-start.13 = (bf16[128,768]{1,0:T(8,128)(2,1)}, bf16[128,768]{1,0:T(8,128)(2,1)S(1)}, u32[]{:S(2)}) copy-start(bf16[128,768]{1,0:T(8,128)(2,1)S(1)} %fusion.41) | copy-start | bytes 589828
  159.8 5.8 %copy-start.4 = (f32[1024,128]{1,0:T(8,128)}, f32[1024,128]{1,0:T(8,128)S(1)}, u32[]{:S(2)}) copy-start(f32[1024,128]{1,0:T(8,128)S(1)} %get-tuple-element.54) | copy-start | bytes 1572868
  160.6 5.0 %collective-permute-start.2 = (bf16[96,128]{1,0:T(8,128)(2,1)S(1)}, bf16[96,128]{1,0:T(8,128)(2,1)S(1)}, u32[]{:S(2)}, u32[]{:S(2)}) collective-permute-start(bf16[96,128]{1,0:T(8,128)(2,1)S(1)} %get-tuple-element.30), channel_id=1, source_target_pairs={{0,1},{1,2},{2,3},{4,5},{5,6},{6,7},{8,9},{9,10},{10,11},{12,13},{... | collective-permute-start | bytes 73736 | tf_op jit(solution)/shard_map/ppermute | solution.py:28
  164.0 5.7 %collective-permute-start.3 = (bf16[96,128]{1,0:T(8,128)(2,1)S(1)}, bf16[96,128]{1,0:T(8,128)(2,1)S(1)}, u32[]{:S(2)}, u32[]{:S(2)}) collective-permute-start(bf16[96,128]{1,0:T(8,128)(2,1)S(1)} %get-tuple-element.31), channel_id=1, source_target_pairs={{1,0},{2,1},{3,2},{5,4},{6,5},{7,6},{9,8},{10,9},{11,10},{13,12},{... | collective-permute-start | bytes 73736 | tf_op jit(solution)/shard_map/ppermute | solution.py:31
  176.8 0.7 copy-start.18
  176.8 0.7 copy-start.20
  177.5 4.3 %copy-start.5 = (bf16[32,224,128]{2,1,0:T(8,128)(2,1)S(1)}, bf16[32,224,128]{2,1,0:T(8,128)(2,1)}, u32[]{:S(2)}) copy-start(bf16[32,224,128]{2,1,0:T(8,128)(2,1)} %get-tuple-element.11) | copy-start | bytes 5505028
  184.9 12.2 %copy-start.1 = (bf16[768,2304]{1,0:T(8,128)(2,1)S(1)}, bf16[768,2304]{1,0:T(8,128)(2,1)}, u32[]{:S(2)}) copy-start(bf16[768,2304]{1,0:T(8,128)(2,1)} %param.45) | copy-start | bytes 10616836
  188.7 6.6 %copy-start.16 = (f32[1,3,1024]{2,0,1:T(1,128)S(1)}, f32[1,3,1024]{2,0,1:T(1,128)}, u32[]{:S(2)}) copy-start(f32[1,3,1024]{2,0,1:T(1,128)} %param.27) | copy-start | bytes 36868
  188.7 6.6 %copy-start.26 = (bf16[3,128]{1,0:T(4,128)(2,1)S(1)}, bf16[3,128]{1,0:T(4,128)(2,1)}, u32[]{:S(2)}) copy-start(bf16[3,128]{1,0:T(4,128)(2,1)} %param.51) | copy-start | bytes 2308
Sparse Core Ops, SparseCore 0:
  82.8 39.2 all-gather.2
  123.7 21.6 all-gather.4
where the time goes:
time: 205 us; the launch traced here: 204 us
  local copies, waits for them, and re-layouts  56.3 us (27%)
  waiting for transfers between devices  49.1 us (24%)
  matrix products  41.6 us (20%)
  other arithmetic  29 us (14%)
  between operations  15.9 us (8%)
  starting transfers between devices  12 us (6%)
    all_gather x1, waiting for transfers between devices, per_device(): gathered = lax.all_gather(projected[:, D:], 'row', axis=0, tiled=True)  23.7 us
    all_gather x1, waiting for transfers between devices, per_device(): lax.all_gather(pair_bias_of(pair_cond, pair_gain, pair_heads), 'smp', axi...  21.2 us
    slice x4, local copies, waits for them, and re-layouts, window_attend(): windows[:, :, :CA].reshape(block_count, span_rows, AHEADS, head_size)  12.1 us
    sub x2, other arithmetic, softmax_rows(): exponent = jnp.exp(scores - largest)  10.7 us
    another operation x10, local copies, waits for them, and re-layouts, block_spans(): jnp.stack(pieces, axis=1)  10.6 us
    ppermute x2, starting transfers between devices, with_halo(): lax.ppermute(lax.slice_in_dim(block, block.shape[dim] - width, None, axis...  8.95 us
    reduce_sum x6, other arithmetic, layer_norm(): variance = jnp.mean(centred * centred, axis=-1, keepdims=True)  7.22 us
    slice x2, local copies, waits for them, and re-layouts, window_attend(): windows[:, :, CA:].reshape(block_count, span_rows, AHEADS, head_size)  7.01 us
  transfers between devices with their start and end apart: 6, of which 3 were waited for; matrix products, arithmetic and copies ran while one was open for 19% of the time, Pallas kernels for 0%

commit v1 on v0

v1 whole, which is shorter than its diff:
```python
import functools
import jax
import jax.numpy as jnp
from jax import lax
from jax.experimental import pallas as pl
from jax.experimental.pallas import tpu as pltpu
from jax.sharding import PartitionSpec as P

HEADS = 16
AHEADS = 4
WQ = 32
WK = 128
HALO = 96
GQ = 64
HALVES = 2

sigma_data = 16.0
gamma_boost = 0.8
norm_eps = 1e-05
masked_score = -1e30
outside_score = -2e30

f32 = jnp.float32
bf16 = jnp.bfloat16
MESH = pl.DeviceIdType.MESH


def mm(a, b):
    return jnp.dot(a, b, preferred_element_type=f32)


def mm_nt(a, b):
    return lax.dot_general(a, b, (((1,), (1,)), ((), ())), preferred_element_type=f32)


def mm_tn(a, b):
    return lax.dot_general(a, b, (((0,), (0,)), ((), ())), preferred_element_type=f32)


def layer_norm(values, norm_gain):
    average = jnp.mean(values, axis=-1, keepdims=True)
    centred = values - average
    variance = jnp.mean(centred * centred, axis=-1, keepdims=True)
    return centred * lax.rsqrt(variance + norm_eps) * norm_gain


def lanes(shape):
    return lax.broadcasted_iota(jnp.int32, shape, len(shape) - 1)


def kernel(
    n_row, n_smp,
    positions, noise_draw, noise_level, atom_single, token_single, pair_cond,
    atom_to_token, window_offsets, atom_mask, token_mask, coord_in, atom_gain, atom_qkv,
    atom_proj, gather_in, noise_embed, pair_gain, pair_heads, token_gain, token_qkv,
    token_proj, ffn_in, ffn_out, scatter_out, out_gain, coord_out,
    token_out, direction,
    pair_v, qkv_v, proj_v, fin_v, fout_v,
    spread_heads, bias_all, next_all, q_atom, kv_atom, halo_n, halo_o, mixed_atom, state,
    tokens_all, k_all, v_all, q_tok, mixed_tok, token_state, mask_rows,
    w_sem, pair_sem, halo_send, halo_recv, tok_right, tok_left, tok_recv,
    bias_sx, bias_sib, bias_recv,
):
    row = lax.axis_index("row")
    smp = lax.axis_index("smp")
    cores = 2 if n_smp % 2 == 0 else 1
    n_x = n_smp // cores
    my_x, my_c = smp // cores, smp % cores
    atom_rows, ca = atom_single.shape
    tok_rows, d_model = token_single.shape
    ff = fout_v.shape[0]
    key_count = tok_rows * n_row
    j_keys = pair_cond.shape[1]
    half_rows = tok_rows // HALVES
    head_size = d_model // HEADS
    mask_tiles = atom_rows // 128

    loads = [
        pltpu.make_async_copy(token_qkv, qkv_v, w_sem.at[0]),
        pltpu.make_async_copy(token_proj, proj_v, w_sem.at[1]),
        pltpu.make_async_copy(ffn_in, fin_v, w_sem.at[2]),
        pltpu.make_async_copy(ffn_out, fout_v, w_sem.at[3]),
    ]
    pair_loads = [
        pltpu.make_async_copy(
            pair_cond.at[pl.ds(half * half_rows, half_rows)],
            pair_v.at[pl.ds(half * half_rows, half_rows)],
            pair_sem.at[half],
        )
        for half in range(HALVES)
    ]
    pair_loads[0].start()
    pair_loads[1].start()
    for load in loads:
        load.start()

    barrier = pltpu.get_barrier_semaphore()
    smp_peers = [((my_x + d) % n_x) * cores + my_c for d in range(1, n_x)]
    if cores == 2:
        smp_peers.append(my_x * cores + (1 - my_c))
    for peer in smp_peers:
        pl.semaphore_signal(barrier, inc=1, device_id={"smp": peer}, device_id_type=MESH)

    @pl.when(row > 0)
    def _():
        pl.semaphore_signal(barrier, inc=1, device_id={"row": row - 1}, device_id_type=MESH)

    @pl.when(row < n_row - 1)
    def _():
        pl.semaphore_signal(barrier, inc=1, device_id={"row": row + 1}, device_id_type=MESH)

    has_left = (row + n_row - 1) // n_row
    has_right = (2 * n_row - 2 - row) // n_row


    def halo_copies(phase):
        right = pltpu.make_async_remote_copy(
            src_ref=next_all.at[phase, pl.ds(atom_rows - HALO, HALO)],
            dst_ref=halo_n.at[phase, 0],
            send_sem=halo_send.at[phase, 0],
            recv_sem=halo_recv.at[phase, 0],
            device_id={"row": row + 1},
            device_id_type=MESH,
        )
        left = pltpu.make_async_remote_copy(
            src_ref=next_all.at[phase, pl.ds(0, HALO)],
            dst_ref=halo_n.at[phase, 1],
            send_sem=halo_send.at[phase, 1],
            recv_sem=halo_recv.at[phase, 1],
            device_id={"row": row - 1},
            device_id_type=MESH,
        )
        return right, left

    def halo_start(phase):
        right, left = halo_copies(phase)

        @pl.when(row < n_row - 1)
        def _():
            right.start()

        @pl.when(row > 0)
        def _():
            left.start()

    def halo_finish(phase, w_kv):
        right, left = halo_copies(phase)
        for side, here, copy, base in (
            (0, row > 0, right, 0),
            (1, row < n_row - 1, left, HALO + atom_rows),
        ):

            @pl.when(here)
            def _():
                copy.wait_recv()
                kv_atom[pl.ds(base, HALO), :] = mm(halo_n[phase, side], w_kv).astype(bf16)

            @pl.when(jnp.logical_not(here))
            def _():
                kv_atom[pl.ds(base, HALO), :] = jnp.zeros((HALO, 2 * ca), bf16)

        @pl.when(row < n_row - 1)
        def _():
            right.wait_send()

        @pl.when(row > 0)
        def _():
            left.wait_send()

    level = noise_level[...]
    level_hat = (1.0 + gamma_boost) * level
    noisy = positions[...] + jnp.sqrt(level_hat * level_hat - level * level) * noise_draw[...]
    scaled = noisy / jnp.sqrt(level_hat * level_hat + sigma_data * sigma_data)
    state[...] = atom_single[...].astype(f32) + lax.dot_general(
        scaled, coord_in[...], (((0,), (0,)), ((), ())),
        precision=lax.Precision.HIGHEST, preferred_element_type=f32,
    )

    def mask_row(tile):
        top = n_row * mask_tiles
        inside = jnp.logical_and(tile >= 0, tile < top)
        safe = jnp.clip(tile, 0, top - 1)
        values = atom_mask[pl.ds(safe, 1), :].astype(f32)
        return jnp.where(inside, values, jnp.zeros_like(values))

    def build_masks(pair, carry):
        tile = row * mask_tiles + pair
        wide = jnp.concatenate(
            [mask_row(tile - 1), mask_row(tile), mask_row(tile + 1), jnp.zeros((1, 128), f32)], axis=1
        )
        wide = jnp.broadcast_to(wide, (8, 512))
        for odd in range(2):
            start = 32 + 64 * odd
            moved = pltpu.roll(wide, 512 - start, 1)
            mask_rows[2 * pair + odd] = moved[:, :256]
        return carry

    lax.fori_loop(0, mask_tiles, build_masks, 0)

    def normalise_and_send(phase):
        next_all[phase] = layer_norm(state[...], atom_gain[pl.ds(phase, 1), :]).astype(bf16)

    normalise_and_send(0)
    pl.semaphore_wait(barrier, len(smp_peers) + has_left + has_right)
    halo_start(0)

    unit = 8
    for i in range(unit):
        pick = lanes((HEADS, 128)) == (
            lax.broadcasted_iota(jnp.int32, (HEADS, 128), 0) * unit + i
        )
        spread_heads[pl.ds(i * 128, 128), :] = mm(
            pair_heads[...], pick.astype(f32).astype(bf16)
        ).astype(bf16)
    mean_matrix = jnp.full((ca, ca), 1.0 / ca, bf16)

    def bias_half(half):
        pair_loads[half].wait()

        def body(step, carry):
            base = half * half_rows + step * 16
            parts = []
            for sub in range(2):
                total = None
                for i in range(unit):
                    x = pair_v[base + sub * unit + i]
                    centred = x.astype(f32) - mm(x, mean_matrix)
                    variance = mm((centred * centred).astype(bf16), mean_matrix)
                    normed = (centred * lax.rsqrt(variance + norm_eps) * pair_gain[...]).astype(bf16)
                    term = mm(normed, spread_heads[pl.ds(i * 128, 128), :])
                    total = term if total is None else total + term
                parts.append(jnp.transpose(total).reshape(HEADS, unit, j_keys))
            both = jnp.concatenate(parts, axis=1).astype(bf16)
            bias_all[smp, half, :, pl.ds(pl.multiple_of(step * 16, 16), 16), :] = both
            return carry

        lax.fori_loop(0, half_rows // 16, body, 0)

    def bias_x(half, d):
        return pltpu.make_async_remote_copy(
            src_ref=bias_all.at[smp, half],
            dst_ref=bias_all.at[smp, half],
            send_sem=bias_sx.at[half, d],
            recv_sem=bias_recv.at[half, smp],
            device_id={"smp": ((my_x + d) % n_x) * cores + my_c},
            device_id_type=MESH,
        )

    def bias_to_sibling(half, d):
        slot = ((my_x + n_x - d) % n_x) * cores + my_c
        return pltpu.make_async_remote_copy(
            src_ref=bias_all.at[slot, half],
            dst_ref=bias_all.at[slot, half],
            send_sem=bias_sib.at[half, d],
            recv_sem=bias_recv.at[half, slot],
            device_id={"smp": my_x * cores + (1 - my_c)},
            device_id_type=MESH,
        )

    def bias_arrival(half, d, core):
        slot = ((my_x + n_x - d) % n_x) * cores + core
        return pltpu.make_async_remote_copy(
            src_ref=bias_all.at[slot, half],
            dst_ref=bias_all.at[slot, half],
            send_sem=bias_sx.at[half, 0],
            recv_sem=bias_recv.at[half, slot],
            device_id={"smp": my_x * cores + (1 - my_c) if cores == 2 else smp},
            device_id_type=MESH,
        )

    def bias_send(half):
        for d in range(1, n_x):
            bias_x(half, d).start()
        if cores == 2:
            bias_to_sibling(half, 0).start()

    def bias_relay(half):
        for d in range(1, n_x):
            bias_arrival(half, d, my_c).wait_recv()
            if cores == 2:
                bias_to_sibling(half, d).start()

    def bias_finish(half):
        for d in range(n_x):
            if cores == 2:
                bias_arrival(half, d, 1 - my_c).wait_recv()
                bias_to_sibling(half, d).wait_send()
            if d:
                bias_x(half, d).wait_send()

    head_of_lane = lanes((GQ, ca)) // (ca // AHEADS)
    atom_scale = 1.0 / float(ca // AHEADS) ** 0.5
    group_count = atom_rows // GQ

    def attend_group(group):
        start = pl.multiple_of(group * GQ, GQ)
        queries = q_atom[pl.ds(start, GQ), :]
        zero = jnp.zeros_like(queries)
        stacked = jnp.concatenate(
            [jnp.where(head_of_lane == h, queries, zero) for h in range(AHEADS)], axis=0
        )
        keys = kv_atom[pl.ds(start, 256), :ca]
        values = kv_atom[pl.ds(start, 256), ca:]
        scores = mm_nt(stacked, keys) * atom_scale
        dead = jnp.where(mask_rows[group] > 0, 0.0, masked_score)
        relative = lanes((8, 256))
        rows = []
        for u in range(GQ // WQ):
            first = window_offsets[group * (GQ // WQ) + u] + (HALO + WQ * u)
            inside = (relative >= first) & (relative < first + WK)
            own = jnp.where(inside, dead, outside_score)
            rows += [own] * (WQ // 8)
        limits = jnp.concatenate(rows, axis=0)
        scores = scores.reshape(AHEADS, GQ, 256) + limits[None]
        scores = scores.reshape(AHEADS * GQ, 256)
        largest = jnp.max(scores, axis=-1, keepdims=True)
        exponent = jnp.exp(scores - largest)
        total = jnp.sum(exponent, axis=-1, keepdims=True)
        mixed = mm(exponent.astype(bf16), values) / total
        result = jnp.zeros((GQ, ca), f32)
        for h in range(AHEADS):
            result = jnp.where(head_of_lane == h, mixed[h * GQ : (h + 1) * GQ], result)
        mixed_atom[pl.ds(start, GQ), :] = result.astype(bf16)

    def atom_block(phase, between):
        w_qkv = atom_qkv[phase]
        projected = mm(next_all[phase], w_qkv).astype(bf16)
        q_atom[...] = projected[:, :ca]
        kv_atom[pl.ds(HALO, atom_rows), :] = projected[:, ca:]
        between()

        def body(group, carry):
            attend_group(group)
            return carry

        lax.fori_loop(2, group_count - 2, body, 0, unroll=2)
        halo_finish(phase, w_qkv[:, ca:])

        def edge(k, carry):
            attend_group(k + (k // 2) * (group_count - 4))
            return carry

        lax.fori_loop(0, 4, edge, 0, unroll=2)
        state[...] = state[...] + mm(mixed_atom[...], atom_proj[phase])

    def first_half():
        bias_half(0)
        bias_send(0)

    atom_block(0, first_half)

    ids = atom_to_token[...] - row * tok_rows
    valid = jnp.concatenate([mask_row(row * mask_tiles + k) for k in range(mask_tiles)], axis=1)
    member = (lax.broadcasted_iota(jnp.int32, (tok_rows, atom_rows), 0) == ids) & (valid > 0)
    onehot32 = member.astype(f32)
    onehot = onehot32.astype(bf16)
    counts = jnp.maximum(jnp.sum(onehot32, axis=1, keepdims=True), 1.0)
    lifted = jnp.maximum(mm(state[...].astype(bf16), gather_in[...]), 0.0).astype(bf16)
    token_state[...] = (
        mm(onehot, lifted) / counts
        + token_single[...].astype(f32)
        + jnp.log(level_hat / sigma_data) / 4.0 * noise_embed[...]
    )
    tokens_all[row] = layer_norm(token_state[...], token_gain[0:1, :]).astype(bf16)

    def token_copy(slot, sem, target):
        return pltpu.make_async_remote_copy(
            src_ref=tokens_all.at[slot],
            dst_ref=tokens_all.at[slot],
            send_sem=sem.at[slot],
            recv_sem=tok_recv.at[slot],
            device_id={"row": target},
            device_id_type=MESH,
        )

    @pl.when(row < n_row - 1)
    def _():
        token_copy(row, tok_right, row + 1).start()

    @pl.when(row > 0)
    def _():
        token_copy(row, tok_left, row - 1).start()

    bias_half(1)
    bias_send(1)
    bias_relay(0)

    def project_keys(slot):
        x = tokens_all[slot]
        base = pl.multiple_of(slot * tok_rows, tok_rows)
        k_all[pl.ds(base, tok_rows), :] = mm(x, qkv_v[:, d_model : 2 * d_model]).astype(bf16)
        v_all[pl.ds(base, tok_rows), :] = mm(x, qkv_v[:, 2 * d_model :]).astype(bf16)

    loads[0].wait()
    q_tok[...] = mm(tokens_all[row], qkv_v[:, :d_model]).astype(bf16)
    project_keys(row)
    for t in range(1, n_row):

        @pl.when(row >= t)
        def _():
            slot = row - t
            token_copy(slot, tok_left, row - 1).wait_recv()

            @pl.when(row < n_row - 1)
            def _():
                token_copy(slot, tok_right, row + 1).start()

        @pl.when(row + t < n_row)
        def _():
            slot = row + t
            token_copy(slot, tok_right, row + 1).wait_recv()

            @pl.when(row > 0)
            def _():
                token_copy(slot, tok_left, row - 1).start()

        if t == n_row // 2:
            bias_relay(1)

        @pl.when(row >= t)
        def _():
            project_keys(row - t)

        @pl.when(row + t < n_row)
        def _():
            project_keys(row + t)

    bias_finish(0)
    bias_finish(1)

    mixed_tok[...] = jnp.zeros_like(mixed_tok)
    dead_keys = jnp.where(token_mask[...] > 0, 0.0, masked_score)
    token_scale = 1.0 / float(head_size) ** 0.5
    for h in range(HEADS):
        low = min(h * head_size // 128, d_model // 128 - 2) * 128
        window = lanes((tok_rows, 256)) + low
        mine = (window >= h * head_size) & (window < (h + 1) * head_size)
        queries = q_tok[:, low : low + 256]
        queries = jnp.where(mine, queries, jnp.zeros_like(queries))
        bias = jnp.concatenate(
            [bias_all[s, :, h].reshape(tok_rows, j_keys).astype(f32) for s in range(n_smp)], axis=1
        )
        scores = mm_nt(queries, k_all[:, low : low + 256]) * token_scale + bias + dead_keys
        largest = jnp.max(scores, axis=-1, keepdims=True)
        exponent = jnp.exp(scores - largest)
        total = jnp.sum(exponent, axis=-1, keepdims=True)
        mixed = mm(exponent.astype(bf16), v_all[:, low : low + 256]) / total
        mixed_tok[:, low : low + 256] = jnp.where(mine, mixed, mixed_tok[:, low : low + 256])

    loads[1].wait()
    token_state[...] = token_state[...] + mm(mixed_tok[...].astype(bf16), proj_v[...])
    normed = layer_norm(token_state[...], token_gain[1:2, :]).astype(bf16)
    loads[2].wait()
    gate = mm(normed, fin_v[:, :ff])
    active = (gate / (1.0 + jnp.exp(-gate)) * mm(normed, fin_v[:, ff:])).astype(bf16)
    loads[3].wait()
    result = (token_state[...] + mm(active, fout_v[...])).astype(bf16)
    token_out[...] = result
    spread_back = mm(result, scatter_out[...]).astype(bf16)
    state[...] = state[...] + mm_tn(onehot, spread_back)

    normalise_and_send(1)
    halo_start(1)
    atom_block(1, lambda: None)

    normed_out = layer_norm(state[...], out_gain[...]).astype(bf16)
    update = mm_nt(coord_out[...], normed_out)
    base_square = sigma_data * sigma_data + level_hat * level_hat
    skip_scale = sigma_data * sigma_data / base_square
    out_scale = level_hat * sigma_data / jnp.sqrt(base_square)
    denoised = skip_scale * noisy + out_scale * update
    direction[...] = (noisy - denoised) / level_hat

    for slot in range(n_row):

        @pl.when(jnp.logical_and(row < n_row - 1, slot <= row))
        def _():
            token_copy(slot, tok_right, row + 1).wait_send()

        @pl.when(jnp.logical_and(row > 0, slot >= row))
        def _():
            token_copy(slot, tok_left, row - 1).wait_send()


def per_device(n_row, n_smp, *args):
    (
        positions, noise_draw, noise_level, atom_single, token_single, pair_cond,
        atom_to_token, window_offsets, atom_mask, token_mask, coord_in, atom_gain, atom_qkv,
        atom_proj, gather_in, noise_embed, pair_gain, pair_heads, token_gain, token_qkv,
        token_proj, ffn_in, ffn_out, scatter_out, out_gain, coord_out,
    ) = args
    atom_rows, ca = atom_single.shape
    tok_rows, d_model = token_single.shape
    j_keys = pair_cond.shape[1]
    key_count = tok_rows * n_row
    vmem = pl.BlockSpec(memory_space=pltpu.VMEM)
    smem = pl.BlockSpec(memory_space=pltpu.SMEM)
    hbm = pl.BlockSpec(memory_space=pl.ANY)
    operands = (
        positions[0], noise_draw[0], noise_level.reshape(1, 1), atom_single, token_single,
        pair_cond, atom_to_token.reshape(1, -1), window_offsets, atom_mask.reshape(-1, 128),
        token_mask.reshape(1, -1), coord_in, atom_gain, atom_qkv, atom_proj, gather_in,
        noise_embed.reshape(1, -1), pair_gain.reshape(1, -1), pair_heads, token_gain, token_qkv,
        token_proj, ffn_in, ffn_out, scatter_out, out_gain.reshape(1, -1), coord_out,
    )
    specs = [vmem] * len(operands)
    specs[5] = hbm
    specs[7] = smem
    for i in (19, 20, 21, 22):
        specs[i] = hbm
    dma = pltpu.SemaphoreType.DMA
    token_out, direction = pl.pallas_call(
        functools.partial(kernel, n_row, n_smp),
        out_shape=(
            jax.ShapeDtypeStruct((tok_rows, d_model), bf16),
            jax.ShapeDtypeStruct(positions.shape[1:], f32),
        ),
        in_specs=specs,
        out_specs=(vmem, vmem),
        scratch_shapes=[
            pltpu.VMEM(pair_cond.shape, bf16),
            pltpu.VMEM(token_qkv.shape, bf16),
            pltpu.VMEM(token_proj.shape, bf16),
            pltpu.VMEM(ffn_in.shape, bf16),
            pltpu.VMEM(ffn_out.shape, bf16),
            pltpu.VMEM((8 * 128, 128), bf16),
            pltpu.VMEM((n_smp, HALVES, HEADS, tok_rows // HALVES, j_keys), bf16),
            pltpu.VMEM((2, atom_rows, ca), bf16),
            pltpu.VMEM((atom_rows, ca), bf16),
            pltpu.VMEM((atom_rows + 2 * HALO, 2 * ca), bf16),
            pltpu.VMEM((2, 2, HALO, ca), bf16),
            pltpu.VMEM((8, 128), bf16),
            pltpu.VMEM((atom_rows, ca), bf16),
            pltpu.VMEM((atom_rows, ca), f32),
            pltpu.VMEM((n_row, tok_rows, d_model), bf16),
            pltpu.VMEM((key_count, d_model), bf16),
            pltpu.VMEM((key_count, d_model), bf16),
            pltpu.VMEM((tok_rows, d_model), bf16),
            pltpu.VMEM((tok_rows, d_model), f32),
            pltpu.VMEM((tok_rows, d_model), f32),
            pltpu.VMEM((atom_rows // GQ, 8, 256), f32),
            dma((4,)),
            dma((HALVES,)),
            dma((2, 2)),
            dma((2, 2)),
            dma((n_row,)),
            dma((n_row,)),
            dma((n_row,)),
            dma((HALVES, n_smp)),
            dma((HALVES, n_smp)),
            dma((HALVES, n_smp)),
        ],
        compiler_params=pltpu.CompilerParams(
            collective_id=0, has_side_effects=True, vmem_limit_bytes=60 * 1024 * 1024
        ),
    )(*operands)
    return token_out[None], direction[None]


def solution(mesh):
    in_specs = (
        P(("grp", "smp"), None, "row"),
        P(("grp", "smp"), None, "row"),
        P(("grp", "smp")),
        P(("grp", "row"), None),
        P(("grp", "row"), None),
        P(("grp", "row"), "smp", None),
        P(("grp", "row")),
        P(("grp", "row")),
        P("grp"),
        P("grp"),
    ) + (P(),) * 16
    out_specs = (P(("grp", "smp"), "row", None), P(("grp", "smp"), None, "row"))
    return jax.shard_map(
        functools.partial(per_device, mesh.shape["row"], mesh.shape["smp"]),
        mesh=mesh, in_specs=in_specs, out_specs=out_specs, check_vma=False,
    )
```

time: 205 us -> 67.2 us (0.33)
  Pallas kernels: 0 us -> 58.5 us
  local copies, waits for them, and re-layouts: 56.3 us -> 6.95 us
  waiting for transfers between devices: 49.1 us -> 0 us
  matrix products: 41.6 us -> 0 us
  other arithmetic: 29 us -> 0 us
  between operations: 15.9 us -> 1.29 us
  starting transfers between devices: 12 us -> 0 us
    pallas_call x0 -> x1, Pallas kernels: none -> 58.5 us  [per_device(): pl.pallas_call(functools.partial(kernel, n_row, n_smp), out_shape=(jax.Sh...]
    all_gather x2 -> x0, waiting for transfers between devices: 45 us -> none  [the longest x1 23.7 us: per_device(): gathered = lax.all_gather(projected[:, D:], 'row', axis=0, tiled=True)]
    dot_general x18 -> x0, matrix products: 38.3 us -> none  [the longest x1 5.85 us: pair_bias_of(): jnp.einsum('ijc,ch->hij', normed, pair_heads, preferred_element_type=jnp....]
    slice x21 -> x0, local copies, waits for them, and re-layouts: 26.4 us -> none  [the longest x4 12.1 us: window_attend(): windows[:, :, :CA].reshape(block_count, span_rows, AHEADS, head_size)]
    ppermute x4 -> x0, starting transfers between devices: 11.7 us -> none  [the longest x2 8.95 us: with_halo(): lax.ppermute(lax.slice_in_dim(block, block.shape[dim] - width, None, axis...]
    sub x3 -> x0, other arithmetic: 11.4 us -> none  [the longest x2 10.7 us: softmax_rows(): exponent = jnp.exp(scores - largest)]
    reduce_sum x8 -> x0, other arithmetic: 10.9 us -> none  [the longest x6 7.22 us: layer_norm(): variance = jnp.mean(centred * centred, axis=-1, keepdims=True)]
    another operation x10 -> x0, local copies, waits for them, and re-layouts: 10.6 us -> none  [block_spans(): jnp.stack(pieces, axis=1)]
  transfers between devices with their start and end apart: 6 -> 0, of which waited for: 3 -> 0; matrix products, arithmetic and copies ran while one was open for 19% -> 0% of each run, Pallas kernels for 0% -> 0%
where the time goes in v1:
time: 67.2 us; the launch traced here: 66.8 us
  Pallas kernels  58.5 us (87%)
  local copies, waits for them, and re-layouts  6.95 us (10%)
  between operations  1.29 us (2%)
    pallas_call x1, Pallas kernels, per_device(): pl.pallas_call(functools.partial(kernel, n_row, n_smp), out_shape=(jax.Sh...  58.5 us
    unnamed x4, local copies, waits for them, and re-layouts  5.68 us

profile of v1, /device:TPU:0, one launch (start us, length us, event | category | flops | bytes accessed | tf_op | source)
XLA Modules:
  0.0 66.8 jit_solution(16624589774194993686)
XLA Ops:
  1.3 1.3 %reshape.29.noise_embed = f32[1,768]{1,0:T(1,128)} reshape(f32[768]{0:T(1024)} %param.41) | data formatting | bytes 6144 | tf_op jit(solution)/shard_map/reshape | solution.py:503
  2.5 1.4 %copy.28.pair_heads = bf16[128,16]{1,0:T(8,128)(2,1)} copy(bf16[128,16]{0,1:T(8,128)(2,1)} %param.43) | data formatting | bytes 8192 | tf_op args[17]
  3.9 1.3 %copy_bitcast_fusion = (f32[3,1024]{1,0:T(4,128)}, f32[3,1024]{1,0:T(4,128)}) fusion(f32[1,3,1024]{2,0,1:T(1,128)} %param.27, f32[1,3,1024]{2,0,1:T(1,128)} %param.26), kind=kLoop, calls=%fused_computation | loop fusion | bytes 49152
  5.3 58.5 %shard_map.257 = (bf16[128,768]{1,0:T(8,128)(2,1)}, f32[3,1024]{1,0:T(4,128)}) custom-call(f32[3,1024]{1,0:T(4,128)} %get-tuple-element.9.positions, f32[3,1024]{1,0:T(4,128)} %get-tuple-element.8.noise_draw, f32[1,1]{1,0:T(1,128)} %bitcast.12.noise_level, bf16[1024,128]{1,0:T(8,128)(2,1)} %atom_single.1, bf16[128,768]{1,0:T(8,128)(2,1)} %token_single.1, ...), custom_call_target="tpu_custom_call" | custom-call | tf_op jit(solution)/shard_map/pallas_call | solution.py:512
  63.8 1.3 %copy.29 = f32[1,3,1024]{2,0,1:T(1,128)} copy(f32[1,3,1024]{2,1,0:T(4,128)} %bitcast.15) | data formatting | bytes 24576
  65.1 1.6 %copy.36 = bf16[1,128,768]{2,1,0:T(8,128)(2,1)} copy(bf16[1,128,768]{2,1,0:T(8,128)(2,1)} %bitcast.13) | data formatting | bytes 393216

commit v2 on v1

--- a/solution.py
+++ b/solution.py
@@ -46,6 +46,11 @@
 
 def lanes(shape):
     return lax.broadcasted_iota(jnp.int32, shape, len(shape) - 1)
+
+
+def noisy_rows(positions, noise_draw, level_hat, level):
+    kick = jnp.sqrt(level_hat * level_hat - level * level)
+    return [positions[k] + kick * noise_draw[k] for k in range(positions.shape[0])]
 
 
 def kernel(
@@ -153,11 +158,11 @@
             @pl.when(here)
             def _():
                 copy.wait_recv()
-                kv_atom[pl.ds(base, HALO), :] = mm(halo_n[phase, side], w_kv).astype(bf16)
+                kv_atom[pl.ds(base, HALO), : 2 * ca] = mm(halo_n[phase, side], w_kv).astype(bf16)
 
             @pl.when(jnp.logical_not(here))
             def _():
-                kv_atom[pl.ds(base, HALO), :] = jnp.zeros((HALO, 2 * ca), bf16)
+                kv_atom[pl.ds(base, HALO), : 2 * ca] = jnp.zeros((HALO, 2 * ca), bf16)
 
         @pl.when(row < n_row - 1)
         def _():
@@ -169,7 +174,7 @@
 
     level = noise_level[...]
     level_hat = (1.0 + gamma_boost) * level
-    noisy = positions[...] + jnp.sqrt(level_hat * level_hat - level * level) * noise_draw[...]
+    noisy = jnp.concatenate(noisy_rows(positions, noise_draw, level_hat, level), axis=0)
     scaled = noisy / jnp.sqrt(level_hat * level_hat + sigma_data * sigma_data)
     state[...] = atom_single[...].astype(f32) + lax.dot_general(
         scaled, coord_in[...], (((0,), (0,)), ((), ())),
@@ -200,6 +205,7 @@
     def normalise_and_send(phase):
         next_all[phase] = layer_norm(state[...], atom_gain[pl.ds(phase, 1), :]).astype(bf16)
 
+    kv_atom[:, 2 * ca :] = jnp.ones((atom_rows + 2 * HALO, ca), bf16)
     normalise_and_send(0)
     pl.semaphore_wait(barrier, len(smp_peers) + has_left + has_right)
     halo_start(0)
@@ -209,7 +215,7 @@
         pick = lanes((HEADS, 128)) == (
             lax.broadcasted_iota(jnp.int32, (HEADS, 128), 0) * unit + i
         )
-        spread_heads[pl.ds(i * 128, 128), :] = mm(
+        spread_heads[pl.ds(i * 128, 128), :] = mm_tn(
             pair_heads[...], pick.astype(f32).astype(bf16)
         ).astype(bf16)
     mean_matrix = jnp.full((ca, ca), 1.0 / ca, bf16)
@@ -219,16 +225,15 @@
 
         def body(step, carry):
             base = half * half_rows + step * 16
+            x = pair_v[pl.ds(base, 2 * unit)].reshape(2 * unit * j_keys, ca)
+            centred = x.astype(f32) - mm(x, mean_matrix)
+            variance = mm((centred * centred).astype(bf16), mean_matrix)
+            normed = (centred * lax.rsqrt(variance + norm_eps) * pair_gain[...]).astype(bf16)
+            normed = normed.reshape(2 * unit, j_keys, ca)
             parts = []
             for sub in range(2):
-                total = None
-                for i in range(unit):
-                    x = pair_v[base + sub * unit + i]
-                    centred = x.astype(f32) - mm(x, mean_matrix)
-                    variance = mm((centred * centred).astype(bf16), mean_matrix)
-                    normed = (centred * lax.rsqrt(variance + norm_eps) * pair_gain[...]).astype(bf16)
-                    term = mm(normed, spread_heads[pl.ds(i * 128, 128), :])
-                    total = term if total is None else total + term
+                wide = jnp.concatenate([normed[sub * unit + i] for i in range(unit)], axis=1)
+                total = mm(wide, spread_heads[...])
                 parts.append(jnp.transpose(total).reshape(HEADS, unit, j_keys))
             both = jnp.concatenate(parts, axis=1).astype(bf16)
             bias_all[smp, half, :, pl.ds(pl.multiple_of(step * 16, 16), 16), :] = both
@@ -315,8 +320,8 @@
         scores = scores.reshape(AHEADS * GQ, 256)
         largest = jnp.max(scores, axis=-1, keepdims=True)
         exponent = jnp.exp(scores - largest)
-        total = jnp.sum(exponent, axis=-1, keepdims=True)
-        mixed = mm(exponent.astype(bf16), values) / total
+        summed = mm(exponent.astype(bf16), values)
+        mixed = summed[:, :ca] / summed[:, ca:]
         result = jnp.zeros((GQ, ca), f32)
         for h in range(AHEADS):
             result = jnp.where(head_of_lane == h, mixed[h * GQ : (h + 1) * GQ], result)
@@ -326,21 +331,21 @@
         w_qkv = atom_qkv[phase]
         projected = mm(next_all[phase], w_qkv).astype(bf16)
         q_atom[...] = projected[:, :ca]
-        kv_atom[pl.ds(HALO, atom_rows), :] = projected[:, ca:]
+        kv_atom[pl.ds(HALO, atom_rows), : 2 * ca] = projected[:, ca:]
         between()
 
         def body(group, carry):
             attend_group(group)
             return carry
 
-        lax.fori_loop(2, group_count - 2, body, 0, unroll=2)
+        lax.fori_loop(2, group_count - 2, body, 0, unroll=4)
         halo_finish(phase, w_qkv[:, ca:])
 
         def edge(k, carry):
             attend_group(k + (k // 2) * (group_count - 4))
             return carry
 
-        lax.fori_loop(0, 4, edge, 0, unroll=2)
+        lax.fori_loop(0, 4, edge, 0, unroll=4)
         state[...] = state[...] + mm(mixed_atom[...], atom_proj[phase])
 
     def first_half():
@@ -356,10 +361,11 @@
     onehot = onehot32.astype(bf16)
     counts = jnp.maximum(jnp.sum(onehot32, axis=1, keepdims=True), 1.0)
     lifted = jnp.maximum(mm(state[...].astype(bf16), gather_in[...]), 0.0).astype(bf16)
+    embed = jnp.concatenate([noise_embed[k : k + 1, :] for k in range(d_model // 128)], axis=1)
     token_state[...] = (
         mm(onehot, lifted) / counts
         + token_single[...].astype(f32)
-        + jnp.log(level_hat / sigma_data) / 4.0 * noise_embed[...]
+        + jnp.log(level_hat / sigma_data) / 4.0 * embed
     )
     tokens_all[row] = layer_norm(token_state[...], token_gain[0:1, :]).astype(bf16)
 
@@ -465,21 +471,30 @@
 
     normed_out = layer_norm(state[...], out_gain[...]).astype(bf16)
     update = mm_nt(coord_out[...], normed_out)
+    for k in range(coord_out.shape[0]):
+        direction[k] = update[k : k + 1]
+
+    for slot in range(n_row):
+
+        @pl.when(jnp.logical_and(row < n_row - 1, slot <= row))
+        def _():
+            token_copy(slot, tok_right, row + 1).wait_send()
+
+        @pl.when(jnp.logical_and(row > 0, slot >= row))
+        def _():
+            token_copy(slot, tok_left, row - 1).wait_send()
+
+
+def finish(positions, noise_draw, noise_level, result, update, token_out, direction):
+    token_out[...] = result[...]
+    level = noise_level[...]
+    level_hat = (1.0 + gamma_boost) * level
     base_square = sigma_data * sigma_data + level_hat * level_hat
     skip_scale = sigma_data * sigma_data / base_square
     out_scale = level_hat * sigma_data / jnp.sqrt(base_square)
-    denoised = skip_scale * noisy + out_scale * update
-    direction[...] = (noisy - denoised) / level_hat
-
-    for slot in range(n_row):
-
-        @pl.when(jnp.logical_and(row < n_row - 1, slot <= row))
-        def _():
-            token_copy(slot, tok_right, row + 1).wait_send()
-
-        @pl.when(jnp.logical_and(row > 0, slot >= row))
-        def _():
-            token_copy(slot, tok_left, row - 1).wait_send()
+    for k, noisy in enumerate(noisy_rows(positions, noise_draw, level_hat, level)):
+        denoised = skip_scale * noisy + out_scale * update[k]
+        direction[k] = (noisy - denoised) / level_hat
 
 
 def per_device(n_row, n_smp, *args):
@@ -497,10 +512,10 @@
     smem = pl.BlockSpec(memory_space=pltpu.SMEM)
     hbm = pl.BlockSpec(memory_space=pl.ANY)
     operands = (
-        positions[0], noise_draw[0], noise_level.reshape(1, 1), atom_single, token_single,
+        positions.transpose(1, 0, 2), noise_draw.transpose(1, 0, 2), noise_level.reshape(1, 1), atom_single, token_single,
         pair_cond, atom_to_token.reshape(1, -1), window_offsets, atom_mask.reshape(-1, 128),
         token_mask.reshape(1, -1), coord_in, atom_gain, atom_qkv, atom_proj, gather_in,
-        noise_embed.reshape(1, -1), pair_gain.reshape(1, -1), pair_heads, token_gain, token_qkv,
+        noise_embed.reshape(-1, 128), pair_gain.reshape(1, -1), pair_heads.T, token_gain, token_qkv,
         token_proj, ffn_in, ffn_out, scatter_out, out_gain.reshape(1, -1), coord_out,
     )
     specs = [vmem] * len(operands)
@@ -509,12 +524,13 @@
     for i in (19, 20, 21, 22):
         specs[i] = hbm
     dma = pltpu.SemaphoreType.DMA
-    token_out, direction = pl.pallas_call(
+    shapes = (
+        jax.ShapeDtypeStruct((tok_rows, d_model), bf16),
+        jax.ShapeDtypeStruct(operands[0].shape, f32),
+    )
+    result, update = pl.pallas_call(
         functools.partial(kernel, n_row, n_smp),
-        out_shape=(
-            jax.ShapeDtypeStruct((tok_rows, d_model), bf16),
-            jax.ShapeDtypeStruct(positions.shape[1:], f32),
-        ),
+        out_shape=shapes,
         in_specs=specs,
         out_specs=(vmem, vmem),
         scratch_shapes=[
@@ -527,7 +543,7 @@
             pltpu.VMEM((n_smp, HALVES, HEADS, tok_rows // HALVES, j_keys), bf16),
             pltpu.VMEM((2, atom_rows, ca), bf16),
             pltpu.VMEM((atom_rows, ca), bf16),
-            pltpu.VMEM((atom_rows + 2 * HALO, 2 * ca), bf16),
+            pltpu.VMEM((atom_rows + 2 * HALO, 3 * ca), bf16),
             pltpu.VMEM((2, 2, HALO, ca), bf16),
             pltpu.VMEM((8, 128), bf16),
             pltpu.VMEM((atom_rows, ca), bf16),
@@ -554,7 +570,10 @@
             collective_id=0, has_side_effects=True, vmem_limit_bytes=60 * 1024 * 1024
         ),
     )(*operands)
-    return token_out[None], direction[None]
+    token_out, direction = pl.pallas_call(
+        finish, out_shape=shapes, in_specs=[vmem] * 5, out_specs=(vmem, vmem)
+    )(*operands[:3], result, update)
+    return token_out[None], direction.transpose(1, 0, 2)
 
 
 def solution(mesh):

time: 67.2 us -> 46.7 us (0.69)
  Pallas kernels: 58.5 us -> 45.3 us
  local copies, waits for them, and re-layouts: 6.95 us -> 0 us
    pallas_call x1 -> x2, Pallas kernels: 58.5 us -> 45.3 us  [the longest x1 43.6 us: per_device(): pl.pallas_call(functools.partial(kernel, n_row, n_smp), out_shape=shapes,...]
    unnamed x4 -> x0, local copies, waits for them, and re-layouts: 5.68 us -> none
    reshape x1 -> x0, local copies, waits for them, and re-layouts: 1.27 us -> none  [per_device(): noise_embed.reshape(1, -1)]
where the time goes in v2:
time: 46.7 us; the launch traced here: 46.6 us
  Pallas kernels  45.3 us (97%)
  between operations  1.3 us (3%)
    pallas_call x1, Pallas kernels, per_device(): pl.pallas_call(functools.partial(kernel, n_row, n_smp), out_shape=shapes,...  43.6 us
    pallas_call x1, Pallas kernels, per_device(): pl.pallas_call(finish, out_shape=shapes, in_specs=[vmem] * 5, out_specs=(...  1.66 us

profile of v2, /device:TPU:0, one launch (start us, length us, event | category | flops | bytes accessed | tf_op | source)
XLA Modules:
  0.0 46.6 jit_solution(912776429204630239)
XLA Ops:
  1.3 43.6 %shard_map.257 = (bf16[128,768]{1,0:T(8,128)(2,1)}, f32[3,1,1024]{2,1,0:T(1,128)}) custom-call(f32[3,1,1024]{2,1,0:T(1,128)} %bitcast.14, f32[3,1,1024]{2,1,0:T(1,128)} %bitcast.16, f32[1,1]{1,0:T(1,128)} %bitcast.12.noise_level, bf16[1024,128]{1,0:T(8,128)(2,1)} %atom_single.1, bf16[128,768]{1,0:T(8,128)(2,1)} %token_single.1, ...), custom_call_target="tpu_custom_call" | custom-call | tf_op jit(solution)/shard_map/pallas_call | solution.py:531
  44.9 1.7 %shard_map.258 = (bf16[128,768]{1,0:T(8,128)(2,1)}, f32[3,1,1024]{2,1,0:T(1,128)}) custom-call(f32[3,1,1024]{2,1,0:T(1,128)} %bitcast.15, f32[3,1,1024]{2,1,0:T(1,128)} %bitcast.17, f32[1,1]{1,0:T(1,128)} %bitcast.13.noise_level, bf16[128,768]{1,0:T(8,128)(2,1)} %get-tuple-element.6.result, f32[3,1,1024]{2,1,0:T(1,128)} %get-tuple-element.7.update), custom_call_target="tpu_custom_call" | custom-call | tf_op jit(solution)/shard_map/pallas_call | solution.py:573

commit v3 on v2

--- a/solution.py
+++ b/solution.py
@@ -12,7 +12,7 @@
 WK = 128
 HALO = 96
 GQ = 64
-HALVES = 2
+HALVES = 4
 
 sigma_data = 16.0
 gamma_boost = 0.8
@@ -94,8 +94,8 @@
         )
         for half in range(HALVES)
     ]
-    pair_loads[0].start()
-    pair_loads[1].start()
+    for load in pair_loads:
+        load.start()
     for load in loads:
         load.start()
 
@@ -387,9 +387,11 @@
     def _():
         token_copy(row, tok_left, row - 1).start()
 
-    bias_half(1)
-    bias_send(1)
+    for part in range(1, HALVES):
+        bias_half(part)
+        bias_send(part)
     bias_relay(0)
+    relayed = 1
 
     def project_keys(slot):
         x = tokens_all[slot]
@@ -420,8 +422,10 @@
             def _():
                 token_copy(slot, tok_left, row - 1).start()
 
-        if t == n_row // 2:
-            bias_relay(1)
+        share = HALVES if t == n_row - 1 else min(HALVES, 1 + t)
+        for part in range(relayed, share):
+            bias_relay(part)
+        relayed = share
 
         @pl.when(row >= t)
         def _():
@@ -431,8 +435,10 @@
         def _():
             project_keys(row + t)
 
-    bias_finish(0)
-    bias_finish(1)
+    for part in range(relayed, HALVES):
+        bias_relay(part)
+    for part in range(HALVES):
+        bias_finish(part)
 
     mixed_tok[...] = jnp.zeros_like(mixed_tok)
     dead_keys = jnp.where(token_mask[...] > 0, 0.0, masked_score)

time: 46.7 us -> 45.5 us (0.974)
  Pallas kernels: 45.3 us -> 44 us
    pallas_call x1, Pallas kernels: 43.6 us -> 42.4 us  [per_device(): pl.pallas_call(functools.partial(kernel, n_row, n_smp), out_shape=shapes,...]
where the time goes in v3:
time: 45.5 us; the launch traced here: 45.3 us
  Pallas kernels  44 us (97%)
  between operations  1.3 us (3%)
    pallas_call x1, Pallas kernels, per_device(): pl.pallas_call(functools.partial(kernel, n_row, n_smp), out_shape=shapes,...  42.4 us
    pallas_call x1, Pallas kernels, per_device(): pl.pallas_call(finish, out_shape=shapes, in_specs=[vmem] * 5, out_specs=(...  1.66 us

profile of v3, /device:TPU:0, one launch (start us, length us, event | category | flops | bytes accessed | tf_op | source)
XLA Modules:
  0.0 45.3 jit_solution(4551250509542061946)
XLA Ops:
  1.3 42.4 %shard_map.257 = (bf16[128,768]{1,0:T(8,128)(2,1)}, f32[3,1,1024]{2,1,0:T(1,128)}) custom-call(f32[3,1,1024]{2,1,0:T(1,128)} %bitcast.14, f32[3,1,1024]{2,1,0:T(1,128)} %bitcast.16, f32[1,1]{1,0:T(1,128)} %bitcast.12.noise_level, bf16[1024,128]{1,0:T(8,128)(2,1)} %atom_single.1, bf16[128,768]{1,0:T(8,128)(2,1)} %token_single.1, ...), custom_call_target="tpu_custom_call" | custom-call | tf_op jit(solution)/shard_map/pallas_call | solution.py:537
  43.7 1.7 %shard_map.258 = (bf16[128,768]{1,0:T(8,128)(2,1)}, f32[3,1,1024]{2,1,0:T(1,128)}) custom-call(f32[3,1,1024]{2,1,0:T(1,128)} %bitcast.15, f32[3,1,1024]{2,1,0:T(1,128)} %bitcast.17, f32[1,1]{1,0:T(1,128)} %bitcast.13.noise_level, bf16[128,768]{1,0:T(8,128)(2,1)} %get-tuple-element.6.result, f32[3,1,1024]{2,1,0:T(1,128)} %get-tuple-element.7.update), custom_call_target="tpu_custom_call" | custom-call | tf_op jit(solution)/shard_map/pallas_call | solution.py:579
